TPU v7x, 256 devices: a whole 4x4x8 slice. The times are simulated.
256 devices in a mesh: section: 8 (over z), expert: 8 (over y_hi, x), dp: 4 (over y_lo, core).
Axes of the slice: x: 4, y: 4 (y_hi: 2, y_lo: 2; y = y_hi * 2 + y_lo), z: 8, core: 2. Of those that a mesh axis runs over, the one named last changes fastest.
Arguments:
- tokens: bfloat16 [8, 256, 4096], P('section', None, ('expert', 'dp'))
- targets: bfloat16 [8, 256, 4096], P('section', None, ('expert', 'dp')), may hold values from -6 to 6
- group_ids: int32 [8, 256], P('section'), may hold values from 0 to 7, as said below
- expert_ids: int32 [1, 8, 8, 256, 2], P(None, 'section'), may hold values from 0 to 7, all different within a row; in each aligned block of 256 rows (0 to 255, 256 to 511, ..., all dimensions but the last counted through in order) at most 72 rows name the same one
- norm_gain: float32 [8, 4096], P('section', ('expert', 'dp')), may hold values from 0.5 to 1.5
- router: bfloat16 [8, 4096, 8], P('section', ('expert', 'dp')), may hold values from -0.09375 to 0.09375
- w_gate: bfloat16 [8, 8, 4096, 1536], P('section', 'expert', None, 'dp'), may hold values from -0.09375 to 0.09375
- w_up: bfloat16 [8, 8, 4096, 1536], P('section', 'expert', None, 'dp'), may hold values from -0.09375 to 0.09375
- w_down: bfloat16 [8, 8, 1536, 4096], P('section', 'expert', 'dp'), may hold values from -0.15625 to 0.15625
Outputs:
- grad_out: bfloat16 [8, 256, 4096], P('section', None, ('expert', 'dp'))
- group_loss: float32 [8], replicated
Inputs may be any that keep to these rules, and one draw needn't show every extreme that they name: `expert_ids`: in each aligned block of 256 rows (one micro-batch at one layer pass) no expert is named by more than 72 rows; a row names 2 different experts. `group_ids`: exactly one group has no rows; which one varies.
All inputs are finite; a program needn't handle non-finite values.
Results may differ from a plain program's by a relative error of at most 0.019.
Values may be sent and summed in bfloat16 or wider, within the bound.
A program may use at most 64 MiB of HBM per device.

v0:
```python
import jax
import jax.numpy as jnp
from jax import lax
from jax.sharding import PartitionSpec as P

GROUPS = 8
dro_rate = 0.3


def from_behind(value, axis, steps):
    count = lax.axis_size(axis)
    pairs = [(source, (source + steps) % count) for source in range(count)]
    return lax.ppermute(value, axis, pairs)


def per_device(tokens, targets, group_ids, expert_ids, norm_gain, router, w_gate, w_up, w_down):
    sections = lax.axis_size("section")
    lane_count = lax.axis_size("dp")
    experts = lax.axis_size("expert")
    circuits = expert_ids.shape[0]
    top_count = expert_ids.shape[-1]
    row_count = tokens.shape[1]
    piece_width = tokens.shape[2]
    full_width = piece_width * experts * lane_count
    capacity = min(row_count, row_count * top_count // experts * 9 // 8)
    section_place = lax.axis_index("section")
    gain_row = norm_gain[0]
    router_block = router[0]
    gate_matrix = w_gate[0, 0]
    up_matrix = w_up[0, 0]
    down_matrix = w_down[0, 0]
    expert_range = jnp.arange(experts, dtype=jnp.int32)
    slot_range = jnp.arange(capacity, dtype=jnp.int32)
    zero_index = jnp.zeros((), jnp.int32)

    def expert_rows(flat_rows):
        gate_part = jnp.dot(flat_rows, gate_matrix, preferred_element_type=jnp.float32)
        up_part = jnp.dot(flat_rows, up_matrix, preferred_element_type=jnp.float32)
        activated = (jax.nn.silu(gate_part) * up_part).astype(jnp.bfloat16)
        return jnp.dot(activated, down_matrix, preferred_element_type=jnp.float32).astype(
            jnp.bfloat16
        )

    def joined_work(received):
        item_count = received.shape[1]
        expert_part = expert_rows(received.reshape(item_count, full_width))
        return lax.all_to_all(
            expert_part.reshape(item_count, experts * lane_count, piece_width),
            ("expert", "dp"),
            split_axis=1,
            concat_axis=1,
            tiled=True,
        )

    def one_tick(moment, current):
        micro_index = (section_place - moment) % sections
        circuit = (moment // sections).astype(jnp.int32)
        choices = lax.dynamic_slice(
            expert_ids,
            (circuit, zero_index, micro_index, zero_index, zero_index),
            (1, 1, 1, row_count, top_count),
        ).reshape(row_count, top_count)
        wide_state = current.astype(jnp.float32)
        local_squares = jnp.sum(wide_state * wide_state, axis=1)
        total_squares = lax.psum(local_squares, ("expert", "dp"))
        row_scale = lax.rsqrt(total_squares / full_width + 1e-06)[:, None]
        normed = (wide_state * row_scale * gain_row[None, :]).astype(jnp.bfloat16)
        partial_logits = jnp.dot(normed, router_block, preferred_element_type=jnp.float32)
        logits = lax.psum(partial_logits, ("expert", "dp"))
        member = (choices[:, :, None] == expert_range[None, None, :]).astype(jnp.int32)
        flat_member = member.reshape(-1, experts)
        rank_before = jnp.cumsum(flat_member, axis=0) - flat_member
        position = jnp.sum(rank_before * flat_member, axis=1).reshape(row_count, top_count)
        chosen = jnp.sum(logits[:, None, :] * member.astype(jnp.float32), axis=2)
        weights = jnp.exp(chosen)
        gate_weights = weights / jnp.sum(weights, axis=1, keepdims=True)
        placement = member.astype(jnp.float32)[:, :, :, None] * (
            position[:, :, None, None] == slot_range[None, None, None, :]
        ).astype(jnp.float32)
        picker = (
            jnp.sum(placement, axis=1).reshape(row_count, experts * capacity).astype(jnp.bfloat16)
        )
        combiner = jnp.sum(placement * gate_weights[:, :, None, None], axis=1)
        outgoing = jnp.einsum(
            "us,ud->sd", picker, normed, preferred_element_type=jnp.float32
        ).astype(jnp.bfloat16)
        spread = jnp.broadcast_to(
            outgoing.reshape(experts, 1, capacity, piece_width),
            (experts, lane_count, capacity, piece_width),
        )
        returned = joined_work(
            lax.all_to_all(
                spread.reshape(experts * lane_count, capacity, piece_width),
                ("expert", "dp"),
                split_axis=0,
                concat_axis=2,
                tiled=True,
            )
        )
        lane_total = jnp.sum(
            returned.reshape(capacity, experts, lane_count, piece_width).astype(jnp.float32), axis=2
        )
        mixture = jnp.einsum("uec,ced->ud", combiner, lane_total, precision=lax.Precision.HIGHEST)
        updated = (wide_state + mixture).astype(jnp.bfloat16)
        return from_behind(updated, "section", 1)

    final_state = lax.fori_loop(0, circuits * sections, one_tick, tokens[0])
    difference = final_state.astype(jnp.float32) - targets[0].astype(jnp.float32)
    partial_squares = jnp.sum(difference * difference, axis=1) / full_width
    group_member = (group_ids[0][:, None] == jnp.arange(GROUPS, dtype=jnp.int32)[None, :]).astype(
        jnp.float32
    )
    local_totals = jnp.dot(partial_squares, group_member, precision=lax.Precision.HIGHEST)
    first_lane = ((lax.axis_index("expert") == 0) & (lax.axis_index("dp") == 0)).astype(jnp.float32)
    local_counts = jnp.sum(group_member, axis=0) * first_lane
    totals, counts = lax.psum((local_totals, local_counts), ("section", "expert", "dp"))
    group_loss = totals / jnp.maximum(counts, 1.0)
    raised = jnp.exp(dro_rate * group_loss)
    group_weight = raised / jnp.sum(raised)
    token_count = sections * row_count
    row_weight_table = group_weight * token_count / jnp.maximum(counts, 1.0)
    row_weight = jnp.dot(group_member, row_weight_table, precision=lax.Precision.HIGHEST)
    grad_out = (row_weight[:, None] * difference).astype(jnp.bfloat16)[None]
    return (grad_out, group_loss)


def solution(mesh):
    placed = (
        P("section", None, ("expert", "dp")),
        P("section", None, ("expert", "dp")),
        P("section", None),
        P(None, "section", None, None, None),
        P("section", ("expert", "dp")),
        P("section", ("expert", "dp"), None),
        P("section", "expert", None, "dp"),
        P("section", "expert", None, "dp"),
        P("section", "expert", "dp", None),
    )
    return jax.shard_map(
        per_device,
        mesh=mesh,
        in_specs=placed,
        out_specs=(P("section", None, ("expert", "dp")), P()),
        check_vma=False,
    )
```

profile of v0, /device:TPU:1, one launch (start us, length us, event | category | flops | bytes accessed | tf_op | source)
XLA Modules:
  0.0 1500.4 jit_solution(1334823001441641367)
XLA Ops:
  2.3 1422.9 %while.17 = (s32[]{:T(128)}, bf16[256,128]{1,0:T(8,128)(2,1)S(1)}, s32[]{:T(128)}, s32[1,1,8,256,2]{3,4,2,1,0:T(2,128)}, f32[1,128]{1,0:T(1,128)}, /*index=5*/bf...) while((s32[]{:T(128)}, bf16[256,128]{1,0:T(8,128)(2,1)S(1)}, ...), condition=%wide.region_12.13_spmd.clone.clone, body=%wide.region_0.12_spmd.clone.clone.sunk | while | flops 947298688 | bytes 33643788 | solution.py:107
  4.3 65.3 %psum.50 = f32[256]{0:T(256)S(1)} all-reduce(f32[256]{0:T(256)S(1)} %fusion.92), channel_id=1, replica_groups=mesh['section'=8,'expert'=8,'dp'=4] {'expert','dp'}, use_global_device_ids=true, to_apply=%region_5.5 | all-reduce | flops 256 | bytes 2048 | tf_op jit(solution)/shard_map/while/body/eval_jaxpr/psum | solution.py:65
  70.4 66.5 %psum.51 = f32[256,8]{0,1:T(8,128)S(1)} all-reduce(f32[256,8]{0,1:T(8,128)S(1)} %fusion.93), channel_id=1, replica_groups=mesh['section'=8,'expert'=8,'dp'=4] {'expert','dp'}, use_global_device_ids=true, to_apply=%region_6.6 | all-reduce | flops 2048 | bytes 16384 | tf_op jit(solution)/shard_map/while/body/eval_jaxpr/psum | solution.py:69
  161.6 16.2 %all_to_all.59 = bf16[72,32,128]{2,0,1:T(8,128)(2,1)S(1)} all-to-all(bf16[72,32,128]{2,0,1:T(8,128)(2,1)S(1)} %bitcast.119), channel_id=1, replica_groups=mesh['section'=8,'expert'=8,'dp'=4] {'expert','dp'}, dimensions={1} | all-to-all | bytes 1179648 | tf_op jit(solution)/shard_map/while/body/eval_jaxpr/all_to_all | solution.py:47
  188.4 63.6 %psum.50 = f32[256]{0:T(256)S(1)} all-reduce(f32[256]{0:T(256)S(1)} %fusion.92), channel_id=1, replica_groups=mesh['section'=8,'expert'=8,'dp'=4] {'expert','dp'}, use_global_device_ids=true, to_apply=%region_5.5 | all-reduce | flops 256 | bytes 2048 | tf_op jit(solution)/shard_map/while/body/eval_jaxpr/psum | solution.py:65
  253.0 63.6 %psum.51 = f32[256,8]{0,1:T(8,128)S(1)} all-reduce(f32[256,8]{0,1:T(8,128)S(1)} %fusion.93), channel_id=1, replica_groups=mesh['section'=8,'expert'=8,'dp'=4] {'expert','dp'}, use_global_device_ids=true, to_apply=%region_6.6 | all-reduce | flops 2048 | bytes 16384 | tf_op jit(solution)/shard_map/while/body/eval_jaxpr/psum | solution.py:69
  365.1 63.9 %psum.50 = f32[256]{0:T(256)S(1)} all-reduce(f32[256]{0:T(256)S(1)} %fusion.92), channel_id=1, replica_groups=mesh['section'=8,'expert'=8,'dp'=4] {'expert','dp'}, use_global_device_ids=true, to_apply=%region_5.5 | all-reduce | flops 256 | bytes 2048 | tf_op jit(solution)/shard_map/while/body/eval_jaxpr/psum | solution.py:65
  430.0 63.6 %psum.51 = f32[256,8]{0,1:T(8,128)S(1)} all-reduce(f32[256,8]{0,1:T(8,128)S(1)} %fusion.93), channel_id=1, replica_groups=mesh['section'=8,'expert'=8,'dp'=4] {'expert','dp'}, use_global_device_ids=true, to_apply=%region_6.6 | all-reduce | flops 2048 | bytes 16384 | tf_op jit(solution)/shard_map/while/body/eval_jaxpr/psum | solution.py:69
  518.2 16.2 %all_to_all.59 = bf16[72,32,128]{2,0,1:T(8,128)(2,1)S(1)} all-to-all(bf16[72,32,128]{2,0,1:T(8,128)(2,1)S(1)} %bitcast.119), channel_id=1, replica_groups=mesh['section'=8,'expert'=8,'dp'=4] {'expert','dp'}, dimensions={1} | all-to-all | bytes 1179648 | tf_op jit(solution)/shard_map/while/body/eval_jaxpr/all_to_all | solution.py:47
  542.1 63.9 %psum.50 = f32[256]{0:T(256)S(1)} all-reduce(f32[256]{0:T(256)S(1)} %fusion.92), channel_id=1, replica_groups=mesh['section'=8,'expert'=8,'dp'=4] {'expert','dp'}, use_global_device_ids=true, to_apply=%region_5.5 | all-reduce | flops 256 | bytes 2048 | tf_op jit(solution)/shard_map/while/body/eval_jaxpr/psum | solution.py:65
  607.0 63.6 %psum.51 = f32[256,8]{0,1:T(8,128)S(1)} all-reduce(f32[256,8]{0,1:T(8,128)S(1)} %fusion.93), channel_id=1, replica_groups=mesh['section'=8,'expert'=8,'dp'=4] {'expert','dp'}, use_global_device_ids=true, to_apply=%region_6.6 | all-reduce | flops 2048 | bytes 16384 | tf_op jit(solution)/shard_map/while/body/eval_jaxpr/psum | solution.py:69
  719.1 63.9 %psum.50 = f32[256]{0:T(256)S(1)} all-reduce(f32[256]{0:T(256)S(1)} %fusion.92), channel_id=1, replica_groups=mesh['section'=8,'expert'=8,'dp'=4] {'expert','dp'}, use_global_device_ids=true, to_apply=%region_5.5 | all-reduce | flops 256 | bytes 2048 | tf_op jit(solution)/shard_map/while/body/eval_jaxpr/psum | solution.py:65
  784.0 63.6 %psum.51 = f32[256,8]{0,1:T(8,128)S(1)} all-reduce(f32[256,8]{0,1:T(8,128)S(1)} %fusion.93), channel_id=1, replica_groups=mesh['section'=8,'expert'=8,'dp'=4] {'expert','dp'}, use_global_device_ids=true, to_apply=%region_6.6 | all-reduce | flops 2048 | bytes 16384 | tf_op jit(solution)/shard_map/while/body/eval_jaxpr/psum | solution.py:69
  872.2 16.2 %all_to_all.59 = bf16[72,32,128]{2,0,1:T(8,128)(2,1)S(1)} all-to-all(bf16[72,32,128]{2,0,1:T(8,128)(2,1)S(1)} %bitcast.119), channel_id=1, replica_groups=mesh['section'=8,'expert'=8,'dp'=4] {'expert','dp'}, dimensions={1} | all-to-all | bytes 1179648 | tf_op jit(solution)/shard_map/while/body/eval_jaxpr/all_to_all | solution.py:47
  896.1 63.9 %psum.50 = f32[256]{0:T(256)S(1)} all-reduce(f32[256]{0:T(256)S(1)} %fusion.92), channel_id=1, replica_groups=mesh['section'=8,'expert'=8,'dp'=4] {'expert','dp'}, use_global_device_ids=true, to_apply=%region_5.5 | all-reduce | flops 256 | bytes 2048 | tf_op jit(solution)/shard_map/while/body/eval_jaxpr/psum | solution.py:65
  960.9 63.6 %psum.51 = f32[256,8]{0,1:T(8,128)S(1)} all-reduce(f32[256,8]{0,1:T(8,128)S(1)} %fusion.93), channel_id=1, replica_groups=mesh['section'=8,'expert'=8,'dp'=4] {'expert','dp'}, use_global_device_ids=true, to_apply=%region_6.6 | all-reduce | flops 2048 | bytes 16384 | tf_op jit(solution)/shard_map/while/body/eval_jaxpr/psum | solution.py:69
  1049.2 16.2 %all_to_all.59 = bf16[72,32,128]{2,0,1:T(8,128)(2,1)S(1)} all-to-all(bf16[72,32,128]{2,0,1:T(8,128)(2,1)S(1)} %bitcast.119), channel_id=1, replica_groups=mesh['section'=8,'expert'=8,'dp'=4] {'expert','dp'}, dimensions={1} | all-to-all | bytes 1179648 | tf_op jit(solution)/shard_map/while/body/eval_jaxpr/all_to_all | solution.py:47
  1073.1 63.9 %psum.50 = f32[256]{0:T(256)S(1)} all-reduce(f32[256]{0:T(256)S(1)} %fusion.92), channel_id=1, replica_groups=mesh['section'=8,'expert'=8,'dp'=4] {'expert','dp'}, use_global_device_ids=true, to_apply=%region_5.5 | all-reduce | flops 256 | bytes 2048 | tf_op jit(solution)/shard_map/while/body/eval_jaxpr/psum | solution.py:65
  1137.9 63.6 %psum.51 = f32[256,8]{0,1:T(8,128)S(1)} all-reduce(f32[256,8]{0,1:T(8,128)S(1)} %fusion.93), channel_id=1, replica_groups=mesh['section'=8,'expert'=8,'dp'=4] {'expert','dp'}, use_global_device_ids=true, to_apply=%region_6.6 | all-reduce | flops 2048 | bytes 16384 | tf_op jit(solution)/shard_map/while/body/eval_jaxpr/psum | solution.py:69
  1226.2 16.2 %all_to_all.59 = bf16[72,32,128]{2,0,1:T(8,128)(2,1)S(1)} all-to-all(bf16[72,32,128]{2,0,1:T(8,128)(2,1)S(1)} %bitcast.119), channel_id=1, replica_groups=mesh['section'=8,'expert'=8,'dp'=4] {'expert','dp'}, dimensions={1} | all-to-all | bytes 1179648 | tf_op jit(solution)/shard_map/while/body/eval_jaxpr/all_to_all | solution.py:47
  1250.1 63.9 %psum.50 = f32[256]{0:T(256)S(1)} all-reduce(f32[256]{0:T(256)S(1)} %fusion.92), channel_id=1, replica_groups=mesh['section'=8,'expert'=8,'dp'=4] {'expert','dp'}, use_global_device_ids=true, to_apply=%region_5.5 | all-reduce | flops 256 | bytes 2048 | tf_op jit(solution)/shard_map/while/body/eval_jaxpr/psum | solution.py:65
  1314.9 63.6 %psum.51 = f32[256,8]{0,1:T(8,128)S(1)} all-reduce(f32[256,8]{0,1:T(8,128)S(1)} %fusion.93), channel_id=1, replica_groups=mesh['section'=8,'expert'=8,'dp'=4] {'expert','dp'}, use_global_device_ids=true, to_apply=%region_6.6 | all-reduce | flops 2048 | bytes 16384 | tf_op jit(solution)/shard_map/while/body/eval_jaxpr/psum | solution.py:69
  1403.2 16.2 %all_to_all.59 = bf16[72,32,128]{2,0,1:T(8,128)(2,1)S(1)} all-to-all(bf16[72,32,128]{2,0,1:T(8,128)(2,1)S(1)} %bitcast.119), channel_id=1, replica_groups=mesh['section'=8,'expert'=8,'dp'=4] {'expert','dp'}, dimensions={1} | all-to-all | bytes 1179648 | tf_op jit(solution)/shard_map/while/body/eval_jaxpr/all_to_all | solution.py:47
  1425.4 72.8 %all-reduce = (f32[8]{0:T(128)S(1)}, f32[8]{0:T(128)S(1)}) all-reduce(f32[8]{0:T(128)S(1)} %broadcast_multiply_fusion.1, f32[8]{0:T(128)S(1)} %convolution_bitcast_fusion.1), channel_id=1, replica_groups=mesh['section'=8,'expert'=8,'dp'=4] {'section','expert','dp'}, use_global_device_ids=true, to_apply=%region_16.17 | all-reduce | flops 16 | bytes 128 | tf_op jit(solution)/shard_map/psum | solution.py:116
  (297 shorter events, 303.8 us)
Async XLA Ops:
  2.3 1422.9 %copy-start.1 = (bf16[1,256,128]{2,1,0:T(8,128)(2,1)S(1)}, bf16[1,256,128]{2,1,0:T(8,128)(2,1)}, u32[]{:S(2)}) copy-start(bf16[1,256,128]{2,1,0:T(8,128)(2,1)} %param.12) | copy-start | bytes 196612
  2.3 1423.0 %copy-start.3 = (s32[1,256]{1,0:T(1,128)S(1)}, s32[1,256]{1,0:T(1,128)}, u32[]{:S(2)}) copy-start(s32[1,256]{1,0:T(1,128)} %param.13) | copy-start | bytes 3076
  138.8 17.4 %copy-start = (bf16[4096,384]{1,0:T(8,128)(2,1)S(1)}, bf16[4096,384]{1,0:T(8,128)(2,1)}, u32[]{:S(2)}) copy-start(bf16[4096,384]{1,0:T(8,128)(2,1)} %get-tuple-element.482) | copy-start | bytes 9437188 | tf_op jit(solution)/shard_map/while
  179.2 7.3 collective-permute-start
  318.4 17.4 %copy-start = (bf16[4096,384]{1,0:T(8,128)(2,1)S(1)}, bf16[4096,384]{1,0:T(8,128)(2,1)}, u32[]{:S(2)}) copy-start(bf16[4096,384]{1,0:T(8,128)(2,1)} %get-tuple-element.482) | copy-start | bytes 9437188 | tf_op jit(solution)/shard_map/while
  358.8 4.4 collective-permute-start
  495.4 17.4 %copy-start = (bf16[4096,384]{1,0:T(8,128)(2,1)S(1)}, bf16[4096,384]{1,0:T(8,128)(2,1)}, u32[]{:S(2)}) copy-start(bf16[4096,384]{1,0:T(8,128)(2,1)} %get-tuple-element.482) | copy-start | bytes 9437188 | tf_op jit(solution)/shard_map/while
  535.8 4.4 collective-permute-start
  672.4 17.4 %copy-start = (bf16[4096,384]{1,0:T(8,128)(2,1)S(1)}, bf16[4096,384]{1,0:T(8,128)(2,1)}, u32[]{:S(2)}) copy-start(bf16[4096,384]{1,0:T(8,128)(2,1)} %get-tuple-element.482) | copy-start | bytes 9437188 | tf_op jit(solution)/shard_map/while
  712.8 4.4 collective-permute-start
  849.4 17.4 %copy-start = (bf16[4096,384]{1,0:T(8,128)(2,1)S(1)}, bf16[4096,384]{1,0:T(8,128)(2,1)}, u32[]{:S(2)}) copy-start(bf16[4096,384]{1,0:T(8,128)(2,1)} %get-tuple-element.482) | copy-start | bytes 9437188 | tf_op jit(solution)/shard_map/while
  889.8 4.4 collective-permute-start
  1026.4 17.4 %copy-start = (bf16[4096,384]{1,0:T(8,128)(2,1)S(1)}, bf16[4096,384]{1,0:T(8,128)(2,1)}, u32[]{:S(2)}) copy-start(bf16[4096,384]{1,0:T(8,128)(2,1)} %get-tuple-element.482) | copy-start | bytes 9437188 | tf_op jit(solution)/shard_map/while
  1066.8 4.4 collective-permute-start
  1203.4 17.4 %copy-start = (bf16[4096,384]{1,0:T(8,128)(2,1)S(1)}, bf16[4096,384]{1,0:T(8,128)(2,1)}, u32[]{:S(2)}) copy-start(bf16[4096,384]{1,0:T(8,128)(2,1)} %get-tuple-element.482) | copy-start | bytes 9437188 | tf_op jit(solution)/shard_map/while
  1243.8 4.4 collective-permute-start
  1380.4 17.4 %copy-start = (bf16[4096,384]{1,0:T(8,128)(2,1)S(1)}, bf16[4096,384]{1,0:T(8,128)(2,1)}, u32[]{:S(2)}) copy-start(bf16[4096,384]{1,0:T(8,128)(2,1)} %get-tuple-element.482) | copy-start | bytes 9437188 | tf_op jit(solution)/shard_map/while
  1420.8 4.4 collective-permute-start
  1498.9 1.5 copy-start.2
where the time goes:
time: 1500 us
  blocking collectives  1350 us (90%)
  matrix products  68.6 us (5%)
  waiting for transfers between devices  35.8 us (2%)
  local copies, waits for them, and re-layouts  20.9 us (1%)
  other arithmetic  16.5 us (1%)
    psum x8, blocking collectives, one_tick(): total_squares = lax.psum(local_squares, ('expert', 'dp'))  512 us
    psum x8, blocking collectives, one_tick(): logits = lax.psum(partial_logits, ('expert', 'dp'))  512 us
    all_to_all x8, blocking collectives, joined_work(): lax.all_to_all(expert_part.reshape(item_count, experts * lane_count, piec...  130 us
    all_to_all x8, blocking collectives, one_tick(): lax.all_to_all(spread.reshape(experts * lane_count, capacity, piece_width...  127 us
    psum x1, blocking collectives, per_device(): lax.psum((local_totals, local_counts), ('section', 'expert', 'dp'))  72.8 us
    ppermute x8, waiting for transfers between devices, from_behind(): return lax.ppermute(value, axis, pairs)  35.8 us
    dot_general x8, matrix products, expert_rows(): jnp.dot(activated, down_matrix, preferred_element_type=jnp.float32)  35.4 us
  transfers between devices with their start and end apart: 8, of which 8 were waited for; matrix products, arithmetic and copies ran while one was open for 0% of the time, Pallas kernels for 0%

commit v1 on v0

--- a/solution.py
+++ b/solution.py
@@ -62,7 +62,7 @@
         ).reshape(row_count, top_count)
         wide_state = current.astype(jnp.float32)
         local_squares = jnp.sum(wide_state * wide_state, axis=1)
-        total_squares = lax.psum(local_squares, ("expert", "dp"))
+        total_squares = lax.psum(lax.psum(local_squares, "dp"), "expert")
         row_scale = lax.rsqrt(total_squares / full_width + 1e-06)[:, None]
         normed = (wide_state * row_scale * gain_row[None, :]).astype(jnp.bfloat16)
         partial_logits = jnp.dot(normed, router_block, preferred_element_type=jnp.float32)

time: 1500 us -> 1210 us (0.81)
  blocking collectives: 1350 us -> 1060 us
    psum x8 -> x16, blocking collectives: 512 us -> 191 us  [one_tick(): total_squares = lax.psum(lax.psum(local_squares, 'dp'), 'expert')]
    psum x8, blocking collectives: 512 us -> 540 us  [one_tick(): logits = lax.psum(partial_logits, ('expert', 'dp'))]
where the time goes in v1:
time: 1210 us
  blocking collectives  1060 us (88%)
  matrix products  68.7 us (6%)
  waiting for transfers between devices  35.8 us (3%)
  local copies, waits for them, and re-layouts  20.9 us (2%)
  other arithmetic  16.5 us (1%)
    psum x8, blocking collectives, one_tick(): logits = lax.psum(partial_logits, ('expert', 'dp'))  540 us
    psum x16, blocking collectives, one_tick(): total_squares = lax.psum(lax.psum(local_squares, 'dp'), 'expert')  191 us
    all_to_all x8, blocking collectives, joined_work(): lax.all_to_all(expert_part.reshape(item_count, experts * lane_count, piec...  130 us
    all_to_all x8, blocking collectives, one_tick(): lax.all_to_all(spread.reshape(experts * lane_count, capacity, piece_width...  127 us
    psum x1, blocking collectives, per_device(): lax.psum((local_totals, local_counts), ('section', 'expert', 'dp'))  72.8 us
    ppermute x8, waiting for transfers between devices, from_behind(): return lax.ppermute(value, axis, pairs)  35.8 us
    dot_general x8, matrix products, expert_rows(): jnp.dot(activated, down_matrix, preferred_element_type=jnp.float32)  35.4 us
  transfers between devices with their start and end apart: 8, of which 8 were waited for; matrix products, arithmetic and copies ran while one was open for 0% of the time, Pallas kernels for 0%

profile of v1, /device:TPU:1, one launch (start us, length us, event | category | flops | bytes accessed | tf_op | source)
XLA Modules:
  0.0 1207.1 jit_solution(6992363134999853861)
XLA Ops:
  2.3 1129.6 %while.17 = (s32[]{:T(128)}, bf16[256,128]{1,0:T(8,128)(2,1)S(1)}, s32[]{:T(128)}, s32[1,1,8,256,2]{3,4,2,1,0:T(2,128)}, f32[1,128]{1,0:T(1,128)}, /*index=5*/bf...) while((s32[]{:T(128)}, bf16[256,128]{1,0:T(8,128)(2,1)S(1)}, ...), condition=%wide.region_13.14_spmd.clone.clone, body=%wide.region_0.13_spmd.clone.clone.sunk | while | flops 947298944 | bytes 33645836 | solution.py:107
  12.5 18.9 %psum.68 = f32[256]{0:T(256)S(1)} all-reduce(f32[256]{0:T(256)S(1)} %psum.67), channel_id=1, replica_groups=mesh['section'=8,'expert'=8,'dp'=4] {'expert'}, use_global_device_ids=true, to_apply=%region_6.6 | all-reduce | flops 256 | bytes 2048 | tf_op jit(solution)/shard_map/while/body/eval_jaxpr/psum | solution.py:65
  32.3 68.4 %psum.69 = f32[256,8]{0,1:T(8,128)S(1)} all-reduce(f32[256,8]{0,1:T(8,128)S(1)} %fusion.93), channel_id=1, replica_groups=mesh['section'=8,'expert'=8,'dp'=4] {'expert','dp'}, use_global_device_ids=true, to_apply=%region_7.7 | all-reduce | flops 2048 | bytes 16384 | tf_op jit(solution)/shard_map/while/body/eval_jaxpr/psum | solution.py:69
  158.7 16.9 %psum.68 = f32[256]{0:T(256)S(1)} all-reduce(f32[256]{0:T(256)S(1)} %psum.67), channel_id=1, replica_groups=mesh['section'=8,'expert'=8,'dp'=4] {'expert'}, use_global_device_ids=true, to_apply=%region_6.6 | all-reduce | flops 256 | bytes 2048 | tf_op jit(solution)/shard_map/while/body/eval_jaxpr/psum | solution.py:65
  176.5 67.2 %psum.69 = f32[256,8]{0,1:T(8,128)S(1)} all-reduce(f32[256,8]{0,1:T(8,128)S(1)} %fusion.93), channel_id=1, replica_groups=mesh['section'=8,'expert'=8,'dp'=4] {'expert','dp'}, use_global_device_ids=true, to_apply=%region_7.7 | all-reduce | flops 2048 | bytes 16384 | tf_op jit(solution)/shard_map/while/body/eval_jaxpr/psum | solution.py:69
  268.3 16.2 %all_to_all.59 = bf16[72,32,128]{2,0,1:T(8,128)(2,1)S(1)} all-to-all(bf16[72,32,128]{2,0,1:T(8,128)(2,1)S(1)} %bitcast.119), channel_id=1, replica_groups=mesh['section'=8,'expert'=8,'dp'=4] {'expert','dp'}, dimensions={1} | all-to-all | bytes 1179648 | tf_op jit(solution)/shard_map/while/body/eval_jaxpr/all_to_all | solution.py:47
  299.1 16.5 %psum.68 = f32[256]{0:T(256)S(1)} all-reduce(f32[256]{0:T(256)S(1)} %psum.67), channel_id=1, replica_groups=mesh['section'=8,'expert'=8,'dp'=4] {'expert'}, use_global_device_ids=true, to_apply=%region_6.6 | all-reduce | flops 256 | bytes 2048 | tf_op jit(solution)/shard_map/while/body/eval_jaxpr/psum | solution.py:65
  316.6 67.4 %psum.69 = f32[256,8]{0,1:T(8,128)S(1)} all-reduce(f32[256,8]{0,1:T(8,128)S(1)} %fusion.93), channel_id=1, replica_groups=mesh['section'=8,'expert'=8,'dp'=4] {'expert','dp'}, use_global_device_ids=true, to_apply=%region_7.7 | all-reduce | flops 2048 | bytes 16384 | tf_op jit(solution)/shard_map/while/body/eval_jaxpr/psum | solution.py:69
  408.5 16.2 %all_to_all.59 = bf16[72,32,128]{2,0,1:T(8,128)(2,1)S(1)} all-to-all(bf16[72,32,128]{2,0,1:T(8,128)(2,1)S(1)} %bitcast.119), channel_id=1, replica_groups=mesh['section'=8,'expert'=8,'dp'=4] {'expert','dp'}, dimensions={1} | all-to-all | bytes 1179648 | tf_op jit(solution)/shard_map/while/body/eval_jaxpr/all_to_all | solution.py:47
  439.4 16.5 %psum.68 = f32[256]{0:T(256)S(1)} all-reduce(f32[256]{0:T(256)S(1)} %psum.67), channel_id=1, replica_groups=mesh['section'=8,'expert'=8,'dp'=4] {'expert'}, use_global_device_ids=true, to_apply=%region_6.6 | all-reduce | flops 256 | bytes 2048 | tf_op jit(solution)/shard_map/while/body/eval_jaxpr/psum | solution.py:65
  456.8 67.4 %psum.69 = f32[256,8]{0,1:T(8,128)S(1)} all-reduce(f32[256,8]{0,1:T(8,128)S(1)} %fusion.93), channel_id=1, replica_groups=mesh['section'=8,'expert'=8,'dp'=4] {'expert','dp'}, use_global_device_ids=true, to_apply=%region_7.7 | all-reduce | flops 2048 | bytes 16384 | tf_op jit(solution)/shard_map/while/body/eval_jaxpr/psum | solution.py:69
  548.8 16.2 %all_to_all.59 = bf16[72,32,128]{2,0,1:T(8,128)(2,1)S(1)} all-to-all(bf16[72,32,128]{2,0,1:T(8,128)(2,1)S(1)} %bitcast.119), channel_id=1, replica_groups=mesh['section'=8,'expert'=8,'dp'=4] {'expert','dp'}, dimensions={1} | all-to-all | bytes 1179648 | tf_op jit(solution)/shard_map/while/body/eval_jaxpr/all_to_all | solution.py:47
  579.6 16.5 %psum.68 = f32[256]{0:T(256)S(1)} all-reduce(f32[256]{0:T(256)S(1)} %psum.67), channel_id=1, replica_groups=mesh['section'=8,'expert'=8,'dp'=4] {'expert'}, use_global_device_ids=true, to_apply=%region_6.6 | all-reduce | flops 256 | bytes 2048 | tf_op jit(solution)/shard_map/while/body/eval_jaxpr/psum | solution.py:65
  597.1 67.4 %psum.69 = f32[256,8]{0,1:T(8,128)S(1)} all-reduce(f32[256,8]{0,1:T(8,128)S(1)} %fusion.93), channel_id=1, replica_groups=mesh['section'=8,'expert'=8,'dp'=4] {'expert','dp'}, use_global_device_ids=true, to_apply=%region_7.7 | all-reduce | flops 2048 | bytes 16384 | tf_op jit(solution)/shard_map/while/body/eval_jaxpr/psum | solution.py:69
  689.1 16.2 %all_to_all.59 = bf16[72,32,128]{2,0,1:T(8,128)(2,1)S(1)} all-to-all(bf16[72,32,128]{2,0,1:T(8,128)(2,1)S(1)} %bitcast.119), channel_id=1, replica_groups=mesh['section'=8,'expert'=8,'dp'=4] {'expert','dp'}, dimensions={1} | all-to-all | bytes 1179648 | tf_op jit(solution)/shard_map/while/body/eval_jaxpr/all_to_all | solution.py:47
  719.9 16.5 %psum.68 = f32[256]{0:T(256)S(1)} all-reduce(f32[256]{0:T(256)S(1)} %psum.67), channel_id=1, replica_groups=mesh['section'=8,'expert'=8,'dp'=4] {'expert'}, use_global_device_ids=true, to_apply=%region_6.6 | all-reduce | flops 256 | bytes 2048 | tf_op jit(solution)/shard_map/while/body/eval_jaxpr/psum | solution.py:65
  737.3 67.4 %psum.69 = f32[256,8]{0,1:T(8,128)S(1)} all-reduce(f32[256,8]{0,1:T(8,128)S(1)} %fusion.93), channel_id=1, replica_groups=mesh['section'=8,'expert'=8,'dp'=4] {'expert','dp'}, use_global_device_ids=true, to_apply=%region_7.7 | all-reduce | flops 2048 | bytes 16384 | tf_op jit(solution)/shard_map/while/body/eval_jaxpr/psum | solution.py:69
  829.3 16.2 %all_to_all.59 = bf16[72,32,128]{2,0,1:T(8,128)(2,1)S(1)} all-to-all(bf16[72,32,128]{2,0,1:T(8,128)(2,1)S(1)} %bitcast.119), channel_id=1, replica_groups=mesh['section'=8,'expert'=8,'dp'=4] {'expert','dp'}, dimensions={1} | all-to-all | bytes 1179648 | tf_op jit(solution)/shard_map/while/body/eval_jaxpr/all_to_all | solution.py:47
  860.2 16.5 %psum.68 = f32[256]{0:T(256)S(1)} all-reduce(f32[256]{0:T(256)S(1)} %psum.67), channel_id=1, replica_groups=mesh['section'=8,'expert'=8,'dp'=4] {'expert'}, use_global_device_ids=true, to_apply=%region_6.6 | all-reduce | flops 256 | bytes 2048 | tf_op jit(solution)/shard_map/while/body/eval_jaxpr/psum | solution.py:65
  877.6 67.4 %psum.69 = f32[256,8]{0,1:T(8,128)S(1)} all-reduce(f32[256,8]{0,1:T(8,128)S(1)} %fusion.93), channel_id=1, replica_groups=mesh['section'=8,'expert'=8,'dp'=4] {'expert','dp'}, use_global_device_ids=true, to_apply=%region_7.7 | all-reduce | flops 2048 | bytes 16384 | tf_op jit(solution)/shard_map/while/body/eval_jaxpr/psum | solution.py:69
  1000.4 16.5 %psum.68 = f32[256]{0:T(256)S(1)} all-reduce(f32[256]{0:T(256)S(1)} %psum.67), channel_id=1, replica_groups=mesh['section'=8,'expert'=8,'dp'=4] {'expert'}, use_global_device_ids=true, to_apply=%region_6.6 | all-reduce | flops 256 | bytes 2048 | tf_op jit(solution)/shard_map/while/body/eval_jaxpr/psum | solution.py:65
  1017.9 67.4 %psum.69 = f32[256,8]{0,1:T(8,128)S(1)} all-reduce(f32[256,8]{0,1:T(8,128)S(1)} %fusion.93), channel_id=1, replica_groups=mesh['section'=8,'expert'=8,'dp'=4] {'expert','dp'}, use_global_device_ids=true, to_apply=%region_7.7 | all-reduce | flops 2048 | bytes 16384 | tf_op jit(solution)/shard_map/while/body/eval_jaxpr/psum | solution.py:69
  1109.8 16.2 %all_to_all.59 = bf16[72,32,128]{2,0,1:T(8,128)(2,1)S(1)} all-to-all(bf16[72,32,128]{2,0,1:T(8,128)(2,1)S(1)} %bitcast.119), channel_id=1, replica_groups=mesh['section'=8,'expert'=8,'dp'=4] {'expert','dp'}, dimensions={1} | all-to-all | bytes 1179648 | tf_op jit(solution)/shard_map/while/body/eval_jaxpr/all_to_all | solution.py:47
  1132.1 72.8 %all-reduce = (f32[8]{0:T(128)S(1)}, f32[8]{0:T(128)S(1)}) all-reduce(f32[8]{0:T(128)S(1)} %broadcast_multiply_fusion.1, f32[8]{0:T(128)S(1)} %convolution_bitcast_fusion.1), channel_id=1, replica_groups=mesh['section'=8,'expert'=8,'dp'=4] {'section','expert','dp'}, use_global_device_ids=true, to_apply=%region_17.18 | all-reduce | flops 16 | bytes 128 | tf_op jit(solution)/shard_map/psum | solution.py:116
  (305 shorter events, 360.1 us)
Async XLA Ops:
  2.3 1129.6 %copy-start.1 = (bf16[1,256,128]{2,1,0:T(8,128)(2,1)S(1)}, bf16[1,256,128]{2,1,0:T(8,128)(2,1)}, u32[]{:S(2)}) copy-start(bf16[1,256,128]{2,1,0:T(8,128)(2,1)} %param.12) | copy-start | bytes 196612
  2.3 1129.7 %copy-start.3 = (s32[1,256]{1,0:T(1,128)S(1)}, s32[1,256]{1,0:T(1,128)}, u32[]{:S(2)}) copy-start(s32[1,256]{1,0:T(1,128)} %param.13) | copy-start | bytes 3076
  102.5 17.4 %copy-start = (bf16[4096,384]{1,0:T(8,128)(2,1)S(1)}, bf16[4096,384]{1,0:T(8,128)(2,1)}, u32[]{:S(2)}) copy-start(bf16[4096,384]{1,0:T(8,128)(2,1)} %get-tuple-element.482) | copy-start | bytes 9437188 | tf_op jit(solution)/shard_map/while
  142.9 7.3 collective-permute-start
  245.5 17.4 %copy-start = (bf16[4096,384]{1,0:T(8,128)(2,1)S(1)}, bf16[4096,384]{1,0:T(8,128)(2,1)}, u32[]{:S(2)}) copy-start(bf16[4096,384]{1,0:T(8,128)(2,1)} %get-tuple-element.482) | copy-start | bytes 9437188 | tf_op jit(solution)/shard_map/while
  285.9 4.4 collective-permute-start
  385.8 17.4 %copy-start = (bf16[4096,384]{1,0:T(8,128)(2,1)S(1)}, bf16[4096,384]{1,0:T(8,128)(2,1)}, u32[]{:S(2)}) copy-start(bf16[4096,384]{1,0:T(8,128)(2,1)} %get-tuple-element.482) | copy-start | bytes 9437188 | tf_op jit(solution)/shard_map/while
  426.1 4.4 collective-permute-start
  526.0 17.4 %copy-start = (bf16[4096,384]{1,0:T(8,128)(2,1)S(1)}, bf16[4096,384]{1,0:T(8,128)(2,1)}, u32[]{:S(2)}) copy-start(bf16[4096,384]{1,0:T(8,128)(2,1)} %get-tuple-element.482) | copy-start | bytes 9437188 | tf_op jit(solution)/shard_map/while
  566.4 4.4 collective-permute-start
  666.3 17.4 %copy-start = (bf16[4096,384]{1,0:T(8,128)(2,1)S(1)}, bf16[4096,384]{1,0:T(8,128)(2,1)}, u32[]{:S(2)}) copy-start(bf16[4096,384]{1,0:T(8,128)(2,1)} %get-tuple-element.482) | copy-start | bytes 9437188 | tf_op jit(solution)/shard_map/while
  706.7 4.4 collective-permute-start
  806.6 17.4 %copy-start = (bf16[4096,384]{1,0:T(8,128)(2,1)S(1)}, bf16[4096,384]{1,0:T(8,128)(2,1)}, u32[]{:S(2)}) copy-start(bf16[4096,384]{1,0:T(8,128)(2,1)} %get-tuple-element.482) | copy-start | bytes 9437188 | tf_op jit(solution)/shard_map/while
  846.9 4.4 collective-permute-start
  946.8 17.4 %copy-start = (bf16[4096,384]{1,0:T(8,128)(2,1)S(1)}, bf16[4096,384]{1,0:T(8,128)(2,1)}, u32[]{:S(2)}) copy-start(bf16[4096,384]{1,0:T(8,128)(2,1)} %get-tuple-element.482) | copy-start | bytes 9437188 | tf_op jit(solution)/shard_map/while
  987.2 4.4 collective-permute-start
  1087.1 17.4 %copy-start = (bf16[4096,384]{1,0:T(8,128)(2,1)S(1)}, bf16[4096,384]{1,0:T(8,128)(2,1)}, u32[]{:S(2)}) copy-start(bf16[4096,384]{1,0:T(8,128)(2,1)} %get-tuple-element.482) | copy-start | bytes 9437188 | tf_op jit(solution)/shard_map/while
  1127.4 4.4 collective-permute-start
  1205.5 1.5 copy-start.2
